TPU v7x, 32 devices: a whole 2x2x4 slice. The times are simulated.
32 devices in a mesh: dp: 8 (over z, x), tensor: 4 (over y, core).
Axes of the slice: x: 2, y: 2, z: 4, core: 2. Of those that a mesh axis runs over, the one named last changes fastest.
Arguments:
- tokens: bfloat16 [32768, 768], P(('dp', 'tensor')), may hold values from -6 to 6
- cotangent: bfloat16 [32768, 768], P(('dp', 'tensor')), may hold values from -26 to 26
- seq_group: int32 [16], P('dp'), may hold values from 0 to 1
- block_slot: int32 [13830], replicated, may hold values from 0 to 20751, as said below
- master: float32 [4, 20752, 128], P('tensor', 'dp'), may hold values from -3 to 3
- first_moment: float32 [4, 20752, 128], P('tensor', 'dp'), may hold values from -1 to 1
- second_moment: float32 [4, 20752, 128], P('tensor', 'dp'), may hold values from 0 to 1, as said below
Outputs:
- output: bfloat16 [32768, 768], P(('dp', 'tensor'))
- input_grad: float32 [32768, 768], P(('dp', 'tensor'))
- group_norms: float32 [16], P('dp')
- new_master: float32 [4, 20752, 128], P('tensor', 'dp')
- new_first: float32 [4, 20752, 128], P('tensor', 'dp')
- new_second: float32 [4, 20752, 128], P('tensor', 'dp')
Inputs may be any that keep to these rules, and one draw needn't show every extreme that they name: `block_slot`: all entries differ; slot s belongs to the owner with dp index s // 2594; one owner holds 2594 blocks. `seq_group`: group ids count within one dp index: sequences of different dp indices never share a group. `second_moment`: Positive.
All inputs are finite; a program needn't handle non-finite values.
Results may differ from a plain program's by a relative error of at most 0.012.
Values may be sent and summed in bfloat16 or wider, within the bound.
No kernel may reach another device: no remote copies, remote signals or barrier semaphores. Data moves between devices by JAX's collectives and lax.ppermute only.
A program may use at most 256 MiB of HBM per device.

v0:
```python
import jax
import jax.numpy as jnp
from jax import lax
from jax.sharding import PartitionSpec as P

HEADS = 12
HD = 64
ROT = 16
FF = 3072


eps_norm = 1e-05
eps_adam = 1e-08
beta_one = 0.5
beta_two = 0.6
root_half = 0.7071067811865476
inv_root_tau = 0.3989422804014327


def rotary_tables(length, rot_dims):
    half_rot = rot_dims // 2
    frequency = 10000.0 ** (-2.0 * jnp.arange(half_rot, dtype=jnp.float32) / rot_dims)
    angles = jnp.arange(length, dtype=jnp.float32)[:, None] * frequency[None, :]
    return (jnp.cos(angles), jnp.sin(angles))


def rotate(features, cosine, sine_table, rot_dims):
    half_rot = rot_dims // 2
    first_half = features[..., :half_rot]
    second_half = features[..., half_rot:rot_dims]
    cos_cols = cosine[:, None, :]
    sin_cols = sine_table[:, None, :]
    return jnp.concatenate(
        [
            first_half * cos_cols - second_half * sin_cols,
            second_half * cos_cols + first_half * sin_cols,
            features[..., rot_dims:],
        ],
        axis=-1,
    )


def unrotate(grad_in, cosine, sine_table, rot_dims):
    half_rot = rot_dims // 2
    first_half = grad_in[..., :half_rot]
    second_half = grad_in[..., half_rot:rot_dims]
    cos_cols = cosine[:, None, :]
    sin_cols = sine_table[:, None, :]
    return jnp.concatenate(
        [
            first_half * cos_cols + second_half * sin_cols,
            second_half * cos_cols - first_half * sin_cols,
            grad_in[..., rot_dims:],
        ],
        axis=-1,
    )


def layer_norm(rows_in):
    row_mean = jnp.mean(rows_in, axis=-1, keepdims=True)
    centred = rows_in - row_mean
    inverse = lax.rsqrt(jnp.mean(centred * centred, axis=-1, keepdims=True) + eps_norm)
    return (centred * inverse, inverse)


def unpack(flat_params, d_model, heads_local, ff_local, width_local):
    inner_width = heads_local * HD
    end_qkv = d_model * 3 * inner_width
    end_out = end_qkv + inner_width * d_model
    end_up = end_out + d_model * ff_local
    end_down = end_up + ff_local * d_model
    return (
        flat_params[:end_qkv].reshape(d_model, 3 * inner_width),
        flat_params[end_qkv:end_out].reshape(inner_width, d_model),
        flat_params[end_out:end_up].reshape(d_model, ff_local),
        flat_params[end_up:end_down].reshape(ff_local, d_model),
        flat_params[end_down:].reshape(4, width_local),
    )


def step_rates(position, d_model, heads_local, head_dim, ff_local, seq_len, ff_all):
    end_qkv = d_model * 3 * heads_local * head_dim
    end_out = end_qkv + heads_local * head_dim * d_model
    end_up = end_out + d_model * ff_local
    end_down = end_up + ff_local * d_model
    matrix_rate = d_model ** (-0.5)
    learn_rate = jnp.where(
        position < end_qkv,
        matrix_rate,
        jnp.where(
            position < end_out,
            (seq_len / (5.0 * d_model)) ** 0.5,
            jnp.where(
                position < end_up,
                matrix_rate,
                jnp.where(position < end_down, ff_all ** (-0.5), 0.1),
            ),
        ),
    )
    weight_decay = jnp.where(position < end_down, 0.1, 0.0)
    return (learn_rate.astype(jnp.float32), weight_decay.astype(jnp.float32))


def adam_update(weight, moment_one, moment_two, gradient, learn_rate, weight_decay):
    new_one = beta_one * moment_one + (1.0 - beta_one) * gradient
    new_two = beta_two * moment_two + (1.0 - beta_two) * gradient * gradient
    new_weight = weight - learn_rate * (
        new_one / (jnp.sqrt(new_two) + eps_adam) + weight_decay * weight
    )
    return (new_weight, new_one, new_two)


def by_sequence(tensor_in, seq_count):
    return tensor_in.reshape(seq_count, -1, tensor_in.shape[-1])


def seq_product(left, right, seq_count):
    return jnp.einsum(
        "sli,slj->sij",
        by_sequence(left, seq_count),
        by_sequence(right, seq_count),
        preferred_element_type=jnp.float32,
    )


def on_device(tokens, cotangent, seq_group, block_slot, master, first_moment, second_moment):
    tensor_count = lax.axis_size("tensor")
    tensor_rank = lax.axis_index("tensor")
    owner_index = lax.axis_index("dp")
    owner_count = lax.axis_size("dp")
    d_model = tokens.shape[1]
    local_rows = tokens.shape[0]
    width_local = d_model // tensor_count
    heads_local = HEADS // tensor_count
    inner_width = heads_local * HD
    ff_local = FF // tensor_count
    seq_count = seq_group.shape[0]
    tok_count = local_rows * tensor_count
    seq_len = tok_count // seq_count
    capacity = master.shape[1]
    block_width = master.shape[2]
    block_count = block_slot.shape[0]
    copies = lax.all_gather(master[0].astype(jnp.bfloat16), "dp", axis=0, tiled=True)
    flat_params = copies[block_slot].reshape(-1)
    w_qkv, w_out, w_up, w_down, norm_local = unpack(
        flat_params, d_model, heads_local, ff_local, width_local
    )
    x_full, norm_rows = (
        lax.all_gather(tokens, "tensor", axis=0, tiled=True),
        lax.all_gather(norm_local.reshape(1, 4 * width_local), "tensor", axis=0, tiled=True),
    )
    norm_full = jnp.transpose(norm_rows.reshape(tensor_count, 4, width_local), (1, 0, 2)).reshape(
        4, d_model
    )
    rows_full = x_full.astype(jnp.float32)
    normed, inverse = layer_norm(rows_full)
    norm_gains = norm_full.astype(jnp.float32)
    first_in = (normed * norm_gains[0] + norm_gains[1]).astype(jnp.bfloat16)
    second_in = (normed * norm_gains[2] + norm_gains[3]).astype(jnp.bfloat16)
    projected = jnp.dot(first_in, w_qkv, preferred_element_type=jnp.float32).reshape(
        seq_count, seq_len, 3, heads_local, HD
    )
    cosine, sine_table = rotary_tables(seq_len, ROT)
    queries = rotate(projected[:, :, 0], cosine, sine_table, ROT).astype(jnp.bfloat16)
    key_rows = rotate(projected[:, :, 1], cosine, sine_table, ROT).astype(jnp.bfloat16)
    values = projected[:, :, 2].astype(jnp.bfloat16)
    block_rows = min(512, seq_len)
    block_total = seq_len // block_rows
    scale_factor = HD ** (-0.5)
    starts = jnp.arange(block_total, dtype=jnp.int32) * block_rows
    key_index = jnp.arange(seq_len, dtype=jnp.int32)

    def scores_of(row_start):
        query_block = lax.dynamic_slice_in_dim(queries, row_start, block_rows, 1)
        scores = (
            jnp.einsum("sqhd,skhd->shqk", query_block, key_rows, preferred_element_type=jnp.float32)
            * scale_factor
        )
        allowed = (row_start + jnp.arange(block_rows, dtype=jnp.int32))[:, None] >= key_index[
            None, :
        ]
        return (jnp.where(allowed, scores, -1e30), query_block)

    def forward_block(row_start):
        scores = scores_of(row_start)[0]
        row_peak = jnp.max(scores, axis=-1, keepdims=True)
        exp_scores = jnp.exp(scores - row_peak)
        row_total = jnp.sum(exp_scores, axis=-1, keepdims=True)
        weights_low = (exp_scores / row_total).astype(jnp.bfloat16)
        mixed_heads = jnp.einsum(
            "shqk,skhd->sqhd", weights_low, values, preferred_element_type=jnp.float32
        )
        return (mixed_heads, row_peak + jnp.log(row_total))

    mixed_heads, log_sums = lax.map(forward_block, starts)
    attended = jnp.moveaxis(mixed_heads, 0, 1).reshape(tok_count, inner_width).astype(jnp.bfloat16)
    hidden_pre = jnp.dot(second_in, w_up, preferred_element_type=jnp.float32)
    hidden_low = jax.nn.gelu(hidden_pre, approximate=False).astype(jnp.bfloat16)
    branch = jnp.dot(attended, w_out, preferred_element_type=jnp.float32) + jnp.dot(
        hidden_low, w_down, preferred_element_type=jnp.float32
    )
    branch_sum = lax.psum_scatter(
        branch.astype(jnp.bfloat16), "tensor", scatter_dimension=0, tiled=True
    ).astype(jnp.float32)
    output = (tokens.astype(jnp.float32) + branch_sum).astype(jnp.bfloat16)
    back_full = lax.all_gather(cotangent, "tensor", axis=0, tiled=True)
    grad_down = seq_product(hidden_low, back_full, seq_count)
    grad_hidden = jnp.dot(back_full, w_down.T, preferred_element_type=jnp.float32)
    cumulative = 0.5 * (1.0 + lax.erf(hidden_pre * root_half))
    density = jnp.exp(-0.5 * hidden_pre * hidden_pre) * inv_root_tau
    grad_pre = (grad_hidden * (cumulative + hidden_pre * density)).astype(jnp.bfloat16)
    grad_up = seq_product(second_in, grad_pre, seq_count)
    second_back = jnp.dot(grad_pre, w_up.T, preferred_element_type=jnp.float32)
    grad_out = seq_product(attended, back_full, seq_count)
    grad_attended = jnp.dot(back_full, w_out.T, preferred_element_type=jnp.float32).astype(
        jnp.bfloat16
    )
    grad_blocks_in = jnp.moveaxis(
        grad_attended.reshape(seq_count, block_total, block_rows, heads_local, HD), 1, 0
    )

    def backward_block(carried, inputs):
        row_start, log_sum, grad_block = inputs
        scores, query_block = scores_of(row_start)
        probs = jnp.exp(scores - log_sum)
        grad_probs = jnp.einsum(
            "sqhd,skhd->shqk", grad_block, values, preferred_element_type=jnp.float32
        )
        row_dot = jnp.sum(probs * grad_probs, axis=-1, keepdims=True)
        grad_scores = (probs * (grad_probs - row_dot)).astype(jnp.bfloat16)
        grad_query = (
            jnp.einsum("shqk,skhd->sqhd", grad_scores, key_rows, preferred_element_type=jnp.float32)
            * scale_factor
        )
        grad_keys = (
            carried[0]
            + jnp.einsum(
                "shqk,sqhd->skhd", grad_scores, query_block, preferred_element_type=jnp.float32
            )
            * scale_factor
        )
        grad_values = carried[1] + jnp.einsum(
            "shqk,sqhd->skhd",
            probs.astype(jnp.bfloat16),
            grad_block,
            preferred_element_type=jnp.float32,
        )
        return ((grad_keys, grad_values), grad_query)

    zero_heads = jnp.zeros((seq_count, seq_len, heads_local, HD), jnp.float32)
    key_value_grads, grad_queries = lax.scan(
        backward_block, (zero_heads, zero_heads), (starts, log_sums, grad_blocks_in)
    )
    grad_queries = jnp.moveaxis(grad_queries, 0, 1).reshape(seq_count, seq_len, heads_local, HD)
    grad_qkv = (
        jnp.stack(
            [
                unrotate(grad_queries, cosine, sine_table, ROT),
                unrotate(key_value_grads[0], cosine, sine_table, ROT),
                key_value_grads[1],
            ],
            axis=2,
        )
        .reshape(tok_count, 3 * inner_width)
        .astype(jnp.bfloat16)
    )
    grad_qkv_w = seq_product(first_in, grad_qkv, seq_count)
    first_back = jnp.dot(grad_qkv, w_qkv.T, preferred_element_type=jnp.float32)
    row_start_local = tensor_rank * local_rows
    first_sum, second_sum = (
        lax.psum_scatter(
            first_back.astype(jnp.bfloat16), "tensor", scatter_dimension=0, tiled=True
        ).astype(jnp.float32),
        lax.psum_scatter(
            second_back.astype(jnp.bfloat16), "tensor", scatter_dimension=0, tiled=True
        ).astype(jnp.float32),
    )
    normed_rows = lax.dynamic_slice_in_dim(normed, row_start_local, local_rows, 0)
    inverse_rows = lax.dynamic_slice_in_dim(inverse, row_start_local, local_rows, 0)
    scaled_first = first_sum * norm_gains[0]
    scaled_second = second_sum * norm_gains[2]
    first_mean = jnp.mean(scaled_first, axis=1, keepdims=True)
    first_cross = jnp.mean(scaled_first * normed_rows, axis=1, keepdims=True)
    second_mean = jnp.mean(scaled_second, axis=1, keepdims=True)
    second_cross = jnp.mean(scaled_second * normed_rows, axis=1, keepdims=True)
    grad_input = (
        cotangent.astype(jnp.float32)
        + inverse_rows * (scaled_first - first_mean - normed_rows * first_cross)
        + inverse_rows * (scaled_second - second_mean - normed_rows * second_cross)
    )
    row_seq = (row_start_local + jnp.arange(local_rows, dtype=jnp.int32)) // seq_len
    row_member = (row_seq[None, :] == jnp.arange(seq_count, dtype=jnp.int32)[:, None]).astype(
        jnp.float32
    )
    partial_sums = jnp.stack(
        [
            jnp.dot(row_member, first_sum * normed_rows, precision=lax.Precision.HIGHEST),
            jnp.dot(row_member, first_sum, precision=lax.Precision.HIGHEST),
            jnp.dot(row_member, second_sum * normed_rows, precision=lax.Precision.HIGHEST),
            jnp.dot(row_member, second_sum, precision=lax.Precision.HIGHEST),
        ],
        axis=1,
    )
    norm_grads = lax.psum_scatter(partial_sums, "tensor", scatter_dimension=2, tiled=True)
    per_seq = jnp.concatenate(
        [
            grad_qkv_w.reshape(seq_count, -1),
            grad_out.reshape(seq_count, -1),
            grad_up.reshape(seq_count, -1),
            grad_down.reshape(seq_count, -1),
            norm_grads.reshape(seq_count, -1),
        ],
        axis=1,
    )
    member = (seq_group[None, :] == jnp.arange(seq_count, dtype=jnp.int32)[:, None]).astype(
        jnp.float32
    )
    group_grads = jnp.dot(member, per_seq, precision=lax.Precision.HIGHEST)
    squares = lax.psum(jnp.sum(group_grads * group_grads, axis=1), "tensor")
    group_norms = jnp.sqrt(squares)
    clip_scale = 1.0 / jnp.maximum(group_norms, 1.0)
    clipped = jnp.dot(clip_scale, group_grads, precision=lax.Precision.HIGHEST)
    grad_rows = clipped.reshape(block_count, block_width)
    slot_total = owner_count * capacity
    slot_block = (
        jnp.full((slot_total,), -1, jnp.int32)
        .at[block_slot]
        .set(jnp.arange(block_count, dtype=jnp.int32))
    )
    my_blocks = lax.dynamic_slice_in_dim(slot_block, owner_index * capacity, capacity)
    summed = lax.psum(grad_rows, "dp")
    owned_grad = jnp.where(my_blocks[:, None] >= 0, summed[jnp.maximum(my_blocks, 0)], 0.0)
    position = (
        jnp.maximum(my_blocks, 0)[:, None] * block_width
        + jnp.arange(block_width, dtype=jnp.int32)[None, :]
    )
    learn_rate, weight_decay = step_rates(position, d_model, heads_local, HD, ff_local, seq_len, FF)
    new_weight, new_one, new_two = adam_update(
        master[0], first_moment[0], second_moment[0], owned_grad, learn_rate, weight_decay
    )
    return (output, grad_input, group_norms, new_weight[None], new_one[None], new_two[None])


def solution(mesh):
    placed = (
        P(("dp", "tensor"), None),
        P(("dp", "tensor"), None),
        P("dp"),
        P(),
        P("tensor", "dp", None),
        P("tensor", "dp", None),
        P("tensor", "dp", None),
    )
    return jax.shard_map(
        on_device,
        mesh=mesh,
        in_specs=placed,
        out_specs=(
            P(("dp", "tensor"), None),
            P(("dp", "tensor"), None),
            P("dp"),
            P("tensor", "dp", None),
            P("tensor", "dp", None),
            P("tensor", "dp", None),
        ),
        check_vma=False,
    )
```

profile of v0, /device:TPU:0, one launch (start us, length us, event | category | flops | bytes accessed | tf_op | source)
XLA Modules:
  0.0 1451.3 jit_solution(10674566761597092681)
XLA Ops:
  17.1 148.8 %all-gather.10.cloned.1.call-done = bf16[1,20752,128]{2,0,1:T(2,128)(2,1)} async-done(((bf16[1,2594,128]{2,0,1:T(2,128)(2,1)}), bf16[1,20752,128]{2,0,1:T(2,128)(2,1)}) %all-gather.10.cloned.1.call-update) | async-done | bytes 5312528 | tf_op jit(solution)/shard_map/all_gather | solution.py:143
  165.9 8.5 copy.115
  174.4 30.7 %gather_fusion = bf16[13830,128]{1,0:T(8,128)(2,1)S(1)} fusion(bf16[20752,128]{1,0:T(8,128)(2,1)} %bitcast.203, s32[14336]{0:T(1024)} %pad_clamp_fusion), kind=kCustom, calls=%fused_computation | custom fusion | bytes 7136280 | tf_op jit(solution)/shard_map/gather | solution.py:144
  234.9 7.9 fusion.36
  250.1 10.0 all-gather.8.cloned.1.call-done
  260.0 6.1 fusion.55
  276.1 163.2 %while.30 = (s32[]{:T(128)}, bf16[4,2,512,3,64]{2,4,3,1,0:T(8,128)(2,1)}, f32[4,2,3,512,1]{3,2,1,4,0:T(4,128)S(1)}, s32[4]{0:T(128)S(1)}, bf16[2,2048,3,64]{1,3,...) while((s32[]{:T(128)}, ...), condition=%wide.region_5.6_spmd.clone.clone, body=%wide.region_2.5_spmd.clone.sunk.clone | while | flops 1687156224 | bytes 96723152 | solution.py:195
  280.0 12.1 fusion.178
  292.1 12.1 fusion.179
  304.2 11.6 fusion.180
  320.8 12.1 fusion.178
  332.9 12.1 fusion.179
  345.0 11.6 fusion.180
  361.6 12.1 fusion.178
  373.7 12.1 fusion.179
  385.8 11.6 fusion.180
  402.4 12.1 fusion.178
  414.5 12.1 fusion.179
  426.6 11.6 fusion.180
  439.3 336.2 %while.31 = (s32[]{:T(128)}, f32[2,2048,3,64]{1,3,2,0:T(8,128)}, f32[2,2048,3,64]{1,3,2,0:T(8,128)}, f32[4,2,512,3,64]{2,4,3,1,0:T(8,128)}, s32[4]{0:T(128)S(1)}...) while((s32[]{:T(128)}, f32[2,2048,3,64]{1,3,2,0:T(8,128)}, ...), condition=%wide.region_9.10_spmd.clone.clone, body=%wide.region_7.9_spmd.clone.sunk.clone | while | flops 4126078464 | bytes 275603712 | solution.py:251
  443.5 11.3 fusion.190
  454.8 12.9 bitcast_add_fusion.7
  467.7 18.1 %multiply_reduce_fusion.4 = (f32[2,3,512]{2,1,0:T(4,128)S(1)}, f32[2,3,512,2048]{3,2,1,0:T(8,128)}) fusion(f32[2,3,512,2048]{3,2,1,0:T(8,128)} %fusion.190, f32[2,3,512]{2,1,0:T(4,128)S(1)} %dynamic-slice_bitcast_fusion.3, pred[512,2048]{1,0:T(8,128)(4,1)S(1)} %iota_compare_fusion.12, bf16[2,2048,3,64]{1,3,2,0:T(8,128)(2,1)} %copy-done.1, ...), kind=kOutput, calls=%fused_computation.22.clone.1.clone | convolution fusion | flops 836760576 | bytes 53370884 | tf_op jit(solution)/shard_map/while/body/eval_jaxpr/sqhd,skhd->shqk/dot_general | solution.py:226
  485.8 17.0 %multiply_convert_fusion.3 = bf16[2,3,512,2048]{3,2,1,0:T(8,128)(2,1)S(1)} fusion(f32[2,3,512,2048]{3,2,1,0:T(8,128)} %get-tuple-element.409, f32[2,3,512,2048]{3,2,1,0:T(8,128)} %fusion.190, f32[2,3,512]{2,1,0:T(4,128)S(1)} %get-tuple-element.410, f32[2,3,512]{2,1,0:T(4,128)S(1)} %dynamic-slice_bitcast_fusion.3, ...), kind=kLoop, calls=%fused_computation.21.clone.1.clone | loop fusion | flops 37748736 | bytes 63987712 | tf_op jit(solution)/shard_map/while/body/eval_jaxpr/convert_element_type | solution.py:230
  512.5 9.5 fusion.191
  526.0 11.3 fusion.190
  537.3 13.8 bitcast_add_fusion.7
  551.1 18.1 %multiply_reduce_fusion.4 = (f32[2,3,512]{2,1,0:T(4,128)S(1)}, f32[2,3,512,2048]{3,2,1,0:T(8,128)}) fusion(f32[2,3,512,2048]{3,2,1,0:T(8,128)} %fusion.190, f32[2,3,512]{2,1,0:T(4,128)S(1)} %dynamic-slice_bitcast_fusion.3, pred[512,2048]{1,0:T(8,128)(4,1)S(1)} %iota_compare_fusion.12, bf16[2,2048,3,64]{1,3,2,0:T(8,128)(2,1)} %copy-done.1, ...), kind=kOutput, calls=%fused_computation.22.clone.1.clone | convolution fusion | flops 836760576 | bytes 53370884 | tf_op jit(solution)/shard_map/while/body/eval_jaxpr/sqhd,skhd->shqk/dot_general | solution.py:226
  569.2 17.0 %multiply_convert_fusion.3 = bf16[2,3,512,2048]{3,2,1,0:T(8,128)(2,1)S(1)} fusion(f32[2,3,512,2048]{3,2,1,0:T(8,128)} %get-tuple-element.409, f32[2,3,512,2048]{3,2,1,0:T(8,128)} %fusion.190, f32[2,3,512]{2,1,0:T(4,128)S(1)} %get-tuple-element.410, f32[2,3,512]{2,1,0:T(4,128)S(1)} %dynamic-slice_bitcast_fusion.3, ...), kind=kLoop, calls=%fused_computation.21.clone.1.clone | loop fusion | flops 37748736 | bytes 63987712 | tf_op jit(solution)/shard_map/while/body/eval_jaxpr/convert_element_type | solution.py:230
  590.8 6.1 bitcast_add_fusion.6
  596.9 9.5 fusion.191
  610.4 11.3 fusion.190
  621.7 13.8 bitcast_add_fusion.7
  635.5 18.1 %multiply_reduce_fusion.4 = (f32[2,3,512]{2,1,0:T(4,128)S(1)}, f32[2,3,512,2048]{3,2,1,0:T(8,128)}) fusion(f32[2,3,512,2048]{3,2,1,0:T(8,128)} %fusion.190, f32[2,3,512]{2,1,0:T(4,128)S(1)} %dynamic-slice_bitcast_fusion.3, pred[512,2048]{1,0:T(8,128)(4,1)S(1)} %iota_compare_fusion.12, bf16[2,2048,3,64]{1,3,2,0:T(8,128)(2,1)} %copy-done.1, ...), kind=kOutput, calls=%fused_computation.22.clone.1.clone | convolution fusion | flops 836760576 | bytes 53370884 | tf_op jit(solution)/shard_map/while/body/eval_jaxpr/sqhd,skhd->shqk/dot_general | solution.py:226
  653.6 17.0 %multiply_convert_fusion.3 = bf16[2,3,512,2048]{3,2,1,0:T(8,128)(2,1)S(1)} fusion(f32[2,3,512,2048]{3,2,1,0:T(8,128)} %get-tuple-element.409, f32[2,3,512,2048]{3,2,1,0:T(8,128)} %fusion.190, f32[2,3,512]{2,1,0:T(4,128)S(1)} %get-tuple-element.410, f32[2,3,512]{2,1,0:T(4,128)S(1)} %dynamic-slice_bitcast_fusion.3, ...), kind=kLoop, calls=%fused_computation.21.clone.1.clone | loop fusion | flops 37748736 | bytes 63987712 | tf_op jit(solution)/shard_map/while/body/eval_jaxpr/convert_element_type | solution.py:230
  675.2 6.1 bitcast_add_fusion.6
  681.3 9.5 fusion.191
  694.8 11.3 fusion.190
  706.1 13.8 bitcast_add_fusion.7
  719.9 18.1 %multiply_reduce_fusion.4 = (f32[2,3,512]{2,1,0:T(4,128)S(1)}, f32[2,3,512,2048]{3,2,1,0:T(8,128)}) fusion(f32[2,3,512,2048]{3,2,1,0:T(8,128)} %fusion.190, f32[2,3,512]{2,1,0:T(4,128)S(1)} %dynamic-slice_bitcast_fusion.3, pred[512,2048]{1,0:T(8,128)(4,1)S(1)} %iota_compare_fusion.12, bf16[2,2048,3,64]{1,3,2,0:T(8,128)(2,1)} %copy-done.1, ...), kind=kOutput, calls=%fused_computation.22.clone.1.clone | convolution fusion | flops 836760576 | bytes 53370884 | tf_op jit(solution)/shard_map/while/body/eval_jaxpr/sqhd,skhd->shqk/dot_general | solution.py:226
  738.0 17.0 %multiply_convert_fusion.3 = bf16[2,3,512,2048]{3,2,1,0:T(8,128)(2,1)S(1)} fusion(f32[2,3,512,2048]{3,2,1,0:T(8,128)} %get-tuple-element.409, f32[2,3,512,2048]{3,2,1,0:T(8,128)} %fusion.190, f32[2,3,512]{2,1,0:T(4,128)S(1)} %get-tuple-element.410, f32[2,3,512]{2,1,0:T(4,128)S(1)} %dynamic-slice_bitcast_fusion.3, ...), kind=kLoop, calls=%fused_computation.21.clone.1.clone | loop fusion | flops 37748736 | bytes 63987712 | tf_op jit(solution)/shard_map/while/body/eval_jaxpr/convert_element_type | solution.py:230
  765.7 9.5 fusion.191
  788.4 9.5 copy.74
  813.7 9.7 fusion.108
  828.9 9.4 convolution_convert_fusion
  840.7 33.3 %fusion.41 = (bf16[4096,768]{1,0:T(8,128)(2,1)}, f32[4096,768]{1,0:T(8,128)S(1)}) fusion(bf16[4096,768]{1,0:T(8,128)(2,1)} %get-tuple-element.243, bf16[768,768]{1,0:T(8,128)(2,1)S(1)} %copy-done.22), kind=kOutput, calls=%fused_computation.59 | convolution fusion | flops 5036310528 | bytes 26345472 | tf_op jit(solution)/shard_map/dot_general | solution.py:197
  874.0 9.2 fusion.47
  885.8 7.0 convolution_convert_fusion.1
  892.8 9.4 convolution_bitcast_fusion.1
  909.1 6.2 constant_dynamic-update-slice_fusion.2
  917.7 12.2 convolution_bitcast_fusion
  929.9 11.5 fusion.107
  946.8 21.3 %reduce-scatter.11.cloned.1.call-done = bf16[1024,768]{1,0:T(8,128)(2,1)} async-done(((bf16[4096,768]{1,0:T(8,128)(2,1)}), bf16[1024,768]{1,0:T(8,128)(2,1)}) %reduce-scatter.11.cloned.1.call-update) | async-done | bytes 1572880 | tf_op jit(solution)/shard_map/reduce_scatter | solution.py:274
  977.0 9.1 add_convert_fusion
  986.1 8.1 copy.103
  1002.3 41.5 %multiply_reduce_fusion.1 = (f32[2]{0:T(128)S(1)}, f32[2,1770240]{1,0:T(2,128)}) fusion(f32[2,1770240]{1,0:T(2,128)} %constant_dynamic-update-slice_fusion, s32[2]{0:T(128)S(1)} %copy-done.37), kind=kOutput, calls=%fused_computation.55 | convolution fusion | flops 92052480 | bytes 28323856 | tf_op jit(solution)/shard_map/dot_general | solution.py:318
  1043.8 6.4 psum.14
  1050.1 119.3 %convolution_reduce_fusion = f32[1770240]{0:T(1024)} fusion(f32[2,1770240]{1,0:T(2,128)} %get-tuple-element.263, f32[2]{0:T(128)S(1)} %sqrt.7), kind=kOutput, calls=%fused_computation.116 | convolution fusion | flops 42485764 | bytes 21242888 | tf_op jit(solution)/shard_map/dot_general | solution.py:322
  1169.4 65.6 %scatter_custom_fusion = s32[20752]{0:T(1024)S(1)} fusion(s32[13830]{0:T(1024)} %copy-done.27, s32[13830]{0:T(1024)S(1)} %iota.92, s32[]{:T(128)} %constant.72.clone.1), kind=kCustom, calls=%fused_computation.158 | custom fusion | bytes 83520 | tf_op jit(solution)/shard_map/scatter | solution.py:328
  1246.7 157.5 %all-reduce.2.cloned.1.call-done = f32[13830,128]{1,0:T(8,128)} async-done(((f32[13830,128]{1,0:T(8,128)}), f32[13830,128]{1,0:T(8,128)}) %all-reduce.2.cloned.1.call-update) | async-done | bytes 7080976 | tf_op jit(solution)/shard_map/psum | solution.py:331
  1404.2 7.7 gather_fusion.1
  1417.1 9.0 copy.86
  1426.1 9.0 copy.88
  1435.1 9.0 copy.87
  (270 shorter events, 193.2 us)
Async XLA Ops:
  7.2 7.7 copy-start.35
  7.2 158.7 %all-gather.10.cloned.1.call-start = ((), (), s32[]{:S(2)}) async-start(), calls=%async_computation.10 | async-start | bytes 11953152 | tf_op jit(solution)/shard_map/all_gather | solution.py:143
  10.8 217.5 %all-gather.6.cloned.1.call-start = ((), (), s32[]{:S(2)}) async-start(), calls=%async_computation.4 | async-start | bytes 7864320 | tf_op jit(solution)/shard_map/all_gather | solution.py:149
  11.6 248.4 %all-gather.8.cloned.1.call-start = ((), (), s32[]{:S(2)}) async-start(), calls=%async_computation.6 | async-start | bytes 7864320 | tf_op jit(solution)/shard_map/all_gather | solution.py:206
  12.3 929.1 %reduce-scatter.9.cloned.1.call-start = ((), (), s32[]{:S(2)}) async-start(), calls=%async_computation.7 | async-start | bytes 7864320 | tf_op jit(solution)/shard_map/reduce_scatter | solution.py:271
  214.3 20.6 %copy-start.31 = (f32[768]{0:T(1024)}, f32[768]{0:T(1024)S(1)}, u32[]{:S(2)}) copy-start(f32[768]{0:T(1024)S(1)} %mul.459) | copy-start | bytes 9220
  214.4 20.5 %copy-start.33 = (f32[768]{0:T(1024)}, f32[768]{0:T(1024)S(1)}, u32[]{:S(2)}) copy-start(f32[768]{0:T(1024)S(1)} %mul.475) | copy-start | bytes 9220
  220.0 6.4 copy-start.16
  225.8 6.4 copy-start.17
  228.3 4.7 copy-start.3
  232.2 2.7 copy-start.36
  234.9 7.9 copy-start.30
  242.8 3.9 copy-start.12
  246.9 13.1 copy-start.18
  269.5 3.6 copy-start.11
  269.5 3.8 copy-start.23
  269.5 3.8 copy-start.25
  273.3 2.8 copy-start.29
  273.3 2.8 copy-start.39
  292.1 12.1 copy-start.7
  332.9 12.1 copy-start.7
  373.7 12.1 copy-start.7
  414.5 12.1 copy-start.7
  439.5 3.3 copy-start.1
  502.9 4.5 copy-start
  512.5 9.5 copy-start.2
  522.0 3.3 copy-start.1
  586.3 4.5 copy-start
  596.9 9.5 copy-start.2
  606.4 3.3 copy-start.1
  670.7 4.5 copy-start
  681.3 9.5 copy-start.2
  690.9 3.3 copy-start.1
  755.1 4.5 copy-start
  765.7 9.5 copy-start.2
  775.6 4.1 copy-start.24
  775.6 4.1 copy-start.26
  788.4 9.5 copy-start.9
  799.1 9.3 slice-start
  801.7 6.7 slice-start.1
  806.5 7.2 slice-start.4
  808.4 5.2 slice-start.5
  838.3 129.8 %reduce-scatter.11.cloned.1.call-start = ((), (), s32[]{:S(2)}) async-start(), calls=%async_computation.8 | async-start | bytes 7864320 | tf_op jit(solution)/shard_map/reduce_scatter | solution.py:274
  838.3 35.7 %slice-start.2 = ((s8[6291456]{0:T(1024)(128)(4,1)}), s8[4194304]{0:T(1024)(128)(4,1)S(1)}, s32[]{:S(2)}) async-start(s8[6291456]{0:T(1024)(128)(4,1)} %bitcast.218), calls=%async_computation.14 | async-start | bytes 8388608
  840.6 33.3 %slice-start.3 = ((s8[6291456]{0:T(1024)(128)(4,1)}), s8[2097152]{0:T(1024)(128)(4,1)S(1)}, s32[]{:S(2)}) async-start(s8[6291456]{0:T(1024)(128)(4,1)} %bitcast.218), calls=%async_computation.15 | async-start | bytes 4194304
  840.7 33.3 %copy-start.20 = (bf16[768,768]{1,0:T(8,128)(2,1)S(1)}, bf16[768,768]{1,0:T(8,128)(2,1)}, u32[]{:S(2)}) copy-start(bf16[768,768]{1,0:T(8,128)(2,1)} %reshape.377) | copy-start | bytes 3538948
  883.2 2.6 copy-start.38
  902.2 5.8 copy-start.15
  909.1 91.2 %reduce-scatter.13.cloned.1.call-start = ((), (), s32[]{:S(2)}) async-start(), calls=%async_computation.11 | async-start | bytes 491520
  909.1 6.2 copy-start.10
  917.7 12.2 copy-start.21
  929.9 11.5 copy-start.28
  946.8 30.2 %copy-start.19 = (bf16[192,768]{1,0:T(8,128)(2,1)S(1)}, bf16[192,768]{1,0:T(8,128)(2,1)}, u32[]{:S(2)}) copy-start(bf16[192,768]{1,0:T(8,128)(2,1)} %reshape.375) | copy-start | bytes 884740
  968.1 3.8 copy-start.6
  976.5 262.1 %reduce-scatter.7.cloned.1.call-start = ((), (), s32[]{:S(2)}) async-start(), calls=%async_computation.5 | async-start | bytes 7864320 | tf_op jit(solution)/shard_map/reduce_scatter | solution.py:202
  994.2 410.0 %all-reduce.2.cloned.1.call-start = ((), (), s32[]{:S(2)}) async-start(), calls=%async_computation.9 | async-start | bytes 14163968 | tf_op jit(solution)/shard_map/psum | solution.py:331
  994.3 8.0 copy-start.37
  1050.1 119.3 %copy-start.40 = (f32[2]{0:T(128)}, f32[2]{0:T(128)S(1)}, u32[]{:S(2)}) copy-start(f32[2]{0:T(128)S(1)} %sqrt.7) | copy-start | bytes 28
  1169.4 65.9 %copy-start.5 = (bf16[1024,768]{1,0:T(8,128)(2,1)S(1)}, bf16[1024,768]{1,0:T(8,128)(2,1)}, u32[]{:S(2)}) copy-start(bf16[1024,768]{1,0:T(8,128)(2,1)} %reduce-scatter.9.cloned.1.call-done) | copy-start | bytes 4718596
  1169.4 65.9 %copy-start.32 = (f32[768]{0:T(1024)S(1)}, f32[768]{0:T(1024)}, u32[]{:S(2)}) copy-start(f32[768]{0:T(1024)} %copy-done.31) | copy-start | bytes 9220
  1169.4 65.9 %copy-start.34 = (f32[768]{0:T(1024)S(1)}, f32[768]{0:T(1024)}, u32[]{:S(2)}) copy-start(f32[768]{0:T(1024)} %copy-done.33) | copy-start | bytes 9220
  1235.3 7.0 dynamic-slice-start
  1238.6 3.6 copy-start.13
  1246.7 165.3 %copy-start.14 = (f32[1,2594,128]{2,0,1:T(1,128)S(1)}, f32[1,2594,128]{2,0,1:T(1,128)}, u32[]{:S(2)}) copy-start(f32[1,2594,128]{2,0,1:T(1,128)} %param.15) | copy-start | bytes 3984388
  (7 other events, 9.8 us)
Sparse Core Ops, SparseCore 0:
  10.9 154.8 all-gather.9
  167.4 44.5 all-gather.5
  213.6 46.4 all-gather.7
  838.4 58.8 reduce-scatter.8
  909.2 58.8 reduce-scatter.10
  976.7 20.7 reduce-scatter.12
  1000.0 58.9 reduce-scatter.6
  1169.5 234.6 all-reduce.1
where the time goes:
time: 1460 us; the launch traced here: 1450 us
  matrix products  624 us (43%)
  waiting for transfers between devices  339 us (23%)
  local copies, waits for them, and re-layouts  273 us (19%)
  other arithmetic  172 us (12%)
  loops' own time  16.5 us (1%)
  between operations  15.2 us (1%)
    psum x1, waiting for transfers between devices, on_device(): summed = lax.psum(grad_rows, 'dp')  158 us
    all_gather x1, waiting for transfers between devices, on_device(): lax.all_gather(master[0].astype(jnp.bfloat16), 'dp', axis=0, tiled=True)  149 us
    dot_general x1, matrix products, on_device(): clipped = jnp.dot(clip_scale, group_grads, precision=lax.Precision.HIGHEST)  119 us
    dot_general x8, matrix products, scores_of(): jnp.einsum('sqhd,skhd->shqk', query_block, key_rows, preferred_element_ty...  93.7 us
    unnamed x100, local copies, waits for them, and re-layouts  83.8 us
    dot_general x4, matrix products, backward_block(): jnp.einsum('sqhd,skhd->shqk', grad_block, values, preferred_element_type=...  72.5 us
    convert_element_type x4, other arithmetic, backward_block(): grad_scores = (probs * (grad_probs - row_dot)).astype(jnp.bfloat16)  68.2 us
    scatter x1, local copies, waits for them, and re-layouts, on_device(): slot_block = jnp.full((slot_total,), -1, jnp.int32).at[block_slot].set(jn...  65.6 us
  transfers between devices with their start and end apart: 8, of which 4 were waited for; matrix products, arithmetic and copies ran while one was open for 31% of the time, Pallas kernels for 0%

commit v1 on v0

v1 whole, which is shorter than its diff:
```python
import functools
import jax
import jax.numpy as jnp
from jax import lax
from jax.experimental import pallas as pl
from jax.experimental.pallas import tpu as pltpu
from jax.sharding import PartitionSpec as P

HEADS = 12
HD = 64
ROT = 16
FF = 3072

eps_norm = 1e-05
eps_adam = 1e-08
beta_one = 0.5
beta_two = 0.6
root_half = 0.7071067811865476
inv_root_tau = 0.3989422804014327
PART = 256
VMEM_BYTES = 60 * 1024 * 1024


def dot_nn(left, right):
    return lax.dot_general(
        left, right, (((1,), (0,)), ((), ())), preferred_element_type=jnp.float32
    )


def dot_nt(left, right):
    return lax.dot_general(
        left, right, (((1,), (1,)), ((), ())), preferred_element_type=jnp.float32
    )


def dot_tn(left, right):
    return lax.dot_general(
        left, right, (((0,), (0,)), ((), ())), preferred_element_type=jnp.float32
    )


def turn_tables(seq_len):
    half = ROT // 2
    frequency = 10000.0 ** (-2.0 * jnp.arange(half, dtype=jnp.float32) / ROT)
    angles = jnp.arange(seq_len, dtype=jnp.float32)[:, None] * frequency[None, :]
    cosine, sine = jnp.cos(angles), jnp.sin(angles)
    rest = HD - ROT
    ones = jnp.ones((seq_len, rest), jnp.float32)
    zeros = jnp.zeros((seq_len, rest), jnp.float32)
    blank = jnp.zeros((seq_len, half), jnp.float32)
    keep = jnp.concatenate([cosine, cosine, ones], axis=1)
    low = jnp.concatenate([sine, blank, zeros], axis=1)
    high = jnp.concatenate([blank, sine, zeros], axis=1)
    return tuple(jnp.tile(t, (1, 128 // HD)) for t in (keep, low, high))


def turn(rows, keep, low, high, sign):
    half = ROT // 2
    pieces = []
    for start in range(0, rows.shape[1], 128):
        piece = rows[:, start : start + 128]
        ahead = pltpu.roll(piece, 128 - half, 1)
        behind = pltpu.roll(piece, half, 1)
        pieces.append(piece * keep + sign * (behind * high - ahead * low))
    return jnp.concatenate(pieces, axis=1)


def norm_rows(rows):
    mean = jnp.mean(rows, axis=-1, keepdims=True)
    centred = rows - mean
    inverse = lax.rsqrt(jnp.mean(centred * centred, axis=-1, keepdims=True) + eps_norm)
    return centred * inverse


def pair_squares(first, second):
    both = first + second
    parts = [both * both, first * first, second * second]
    return jnp.concatenate([jnp.sum(p, axis=0, keepdims=True) for p in parts], axis=0)


def dense_kernel(
    tiles_per_seq, x_ref, g_ref, wqkv_ref, wo_ref, wup_ref, wdn_ref, nrm_ref, keep_ref, low_ref, high_ref,
    q_ref, k_ref, v_ref, do_ref, hb_ref, e2_ref, gwd_ref, gwu_ref, gn_ref, sq_ref,
):
    step = pl.program_id(0)
    seq = step // tiles_per_seq

    @pl.when(step == 0)
    def _():
        gwd_ref[...] = jnp.zeros_like(gwd_ref)
        gwu_ref[...] = jnp.zeros_like(gwu_ref)
        gn_ref[...] = jnp.zeros_like(gn_ref)

    xhat = norm_rows(x_ref[...].astype(jnp.float32))
    first_in = (xhat * nrm_ref[0:1, :] + nrm_ref[1:2, :]).astype(jnp.bfloat16)
    second_in = (xhat * nrm_ref[2:3, :] + nrm_ref[3:4, :]).astype(jnp.bfloat16)
    back = g_ref[...]
    hidden_pre = dot_nn(second_in, wup_ref[...])
    grad_hidden = dot_nt(back, wdn_ref[...])
    cumulative = 0.5 * (1.0 + lax.erf(hidden_pre * root_half))
    density = jnp.exp(-0.5 * hidden_pre * hidden_pre) * inv_root_tau
    hidden = (hidden_pre * cumulative).astype(jnp.bfloat16)
    hb_ref[...] = hidden
    grad_pre = (grad_hidden * (cumulative + hidden_pre * density)).astype(jnp.bfloat16)
    projected = dot_nn(first_in, wqkv_ref[...])
    keep, low, high = keep_ref[...], low_ref[...], high_ref[...]
    q_ref[...] = (turn(projected[:, :PART], keep, low, high, 1.0) * HD ** (-0.5)).astype(jnp.bfloat16)
    k_ref[...] = turn(projected[:, PART : 2 * PART], keep, low, high, 1.0).astype(jnp.bfloat16)
    v_ref[...] = projected[:, 2 * PART :].astype(jnp.bfloat16)
    do_ref[...] = dot_nt(back, wo_ref[...]).astype(jnp.bfloat16)
    gwd_ref[seq] += dot_tn(hidden, back)
    gwu_ref[seq] += dot_tn(second_in, grad_pre)
    second_back = dot_nt(grad_pre, wup_ref[...]).astype(jnp.bfloat16)
    e2_ref[...] = second_back
    second_back = second_back.astype(jnp.float32)
    gn_ref[seq] += jnp.concatenate(
        [
            jnp.sum(second_back * xhat, axis=0, keepdims=True),
            jnp.sum(second_back, axis=0, keepdims=True),
        ],
        axis=0,
    )

    @pl.when(step == pl.num_programs(0) - 1)
    def _():
        sq_ref[...] = pair_squares(gwd_ref[0], gwd_ref[1]) + pair_squares(gwu_ref[0], gwu_ref[1])


def attend_kernel(
    block, heads, q_ref, k_ref, v_ref, do_ref, keep_ref, low_ref, high_ref,
    ao_ref, dq_ref, dk_ref, dv_ref, p_s, m_s, l_s, o_s, dq_s, dk_s, dv_s, qh_s, doh_s,
):
    i = pl.program_id(1)
    last = pl.num_programs(1) - 1

    @pl.when(i == 0)
    def _():
        dk_s[...] = jnp.zeros_like(dk_s)
        dv_s[...] = jnp.zeros_like(dv_s)

    dq_s[...] = jnp.zeros_like(dq_s)
    ao_ref[...] = jnp.zeros_like(ao_ref)
    lane_head = lax.broadcasted_iota(jnp.int32, (block, PART), 1) // HD

    def rows_of(j):
        return pl.ds(pl.multiple_of(j * block, block), block)

    def one_head(h, _):
        mine = lane_head == h
        zero = jnp.zeros((), jnp.bfloat16)
        q_head = jnp.where(mine, q_ref[...], zero)
        qh_s[...] = q_head
        do_head = jnp.where(mine, do_ref[...], zero)
        doh_s[...] = do_head
        scores = dot_nt(q_head, k_ref[rows_of(i), :])
        row = lax.broadcasted_iota(jnp.int32, (block, block), 0)
        col = lax.broadcasted_iota(jnp.int32, (block, block), 1)
        scores = jnp.where(row >= col, scores, -1e30)
        peak = jnp.max(scores, axis=1, keepdims=True)
        probs = jnp.exp(scores - peak)
        l_s[...] = jnp.broadcast_to(jnp.sum(probs, axis=1, keepdims=True), l_s.shape)
        probs = probs.astype(jnp.bfloat16)
        p_s[i] = probs
        m_s[i] = jnp.broadcast_to(peak, m_s.shape[1:])
        m_s[last + 1] = m_s[i]
        o_s[...] = dot_nn(probs, v_ref[rows_of(i), :])

        def ahead(j, _):
            scores = dot_nt(qh_s[...], k_ref[rows_of(j), :])
            before = m_s[last + 1][:, :1]
            peak = jnp.maximum(before, jnp.max(scores, axis=1, keepdims=True))
            fade = jnp.exp(before - peak)
            probs = jnp.exp(scores - peak)
            l_s[...] = l_s[...] * fade + jnp.sum(probs, axis=1, keepdims=True)
            probs = probs.astype(jnp.bfloat16)
            p_s[j] = probs
            wide = jnp.broadcast_to(peak, m_s.shape[1:])
            m_s[j] = wide
            m_s[last + 1] = wide
            o_s[...] = o_s[...] * fade + dot_nn(probs, v_ref[rows_of(j), :])
            return 0

        lax.fori_loop(0, i, ahead, 0)
        inverse = 1.0 / l_s[...]
        out = o_s[...] * inverse[:, :1]
        delta = jnp.sum(doh_s[...].astype(jnp.float32) * out, axis=1, keepdims=True)
        ao_ref[...] = jnp.where(mine, out.astype(jnp.bfloat16), ao_ref[...])
        l_s[...] = inverse
        o_s[:, :128] = jnp.broadcast_to(delta, (block, 128))

        def behind(j, _):
            scale = (jnp.exp(m_s[j] - m_s[last + 1]) * l_s[...])[:, :1]
            grad_out = (doh_s[...].astype(jnp.float32) * scale).astype(jnp.bfloat16)
            grad_probs = dot_nt(grad_out, v_ref[rows_of(j), :])
            probs = p_s[j]
            shift = o_s[:, :1] * scale
            grad_scores = (probs.astype(jnp.float32) * (grad_probs - shift)).astype(jnp.bfloat16)
            part = dot_nn(grad_scores, k_ref[rows_of(j), :])
            dq_s[...] += jnp.where(mine, part, 0.0)
            dk_s[rows_of(j), :] += dot_tn(grad_scores, qh_s[...])
            dv_s[rows_of(j), :] += dot_tn(probs, grad_out)
            return 0

        lax.fori_loop(0, i + 1, behind, 0)
        return 0

    lax.fori_loop(0, heads, one_head, 0)
    here = rows_of(i)
    dq_ref[...] = (
        turn(dq_s[...], keep_ref[here, :], low_ref[here, :], high_ref[here, :], -1.0) * HD ** (-0.5)
    ).astype(jnp.bfloat16)

    @pl.when(i == last)
    def _():
        dk_ref[...] = turn(dk_s[...], keep_ref[...], low_ref[...], high_ref[...], -1.0).astype(jnp.bfloat16)
        dv_ref[...] = dv_s[...].astype(jnp.bfloat16)


def grads_kernel(
    tiles_per_seq, x_ref, g_ref, ao_ref, dq_ref, dk_ref, dv_ref, wqkv_ref, nrm_ref,
    e1_ref, gwq_ref, gwo_ref, gn_ref, sq_ref,
):
    step = pl.program_id(0)
    seq = step // tiles_per_seq

    @pl.when(step == 0)
    def _():
        gwq_ref[...] = jnp.zeros_like(gwq_ref)
        gwo_ref[...] = jnp.zeros_like(gwo_ref)
        gn_ref[...] = jnp.zeros_like(gn_ref)

    xhat = norm_rows(x_ref[...].astype(jnp.float32))
    first_in = (xhat * nrm_ref[0:1, :] + nrm_ref[1:2, :]).astype(jnp.bfloat16)
    grad_qkv = jnp.concatenate([dq_ref[...], dk_ref[...], dv_ref[...]], axis=1)
    first_back = dot_nt(grad_qkv, wqkv_ref[...]).astype(jnp.bfloat16)
    e1_ref[...] = first_back
    gwq_ref[seq] += dot_tn(first_in, grad_qkv)
    gwo_ref[seq] += dot_tn(ao_ref[...], g_ref[...])
    first_back = first_back.astype(jnp.float32)
    gn_ref[seq] += jnp.concatenate(
        [
            jnp.sum(first_back * xhat, axis=0, keepdims=True),
            jnp.sum(first_back, axis=0, keepdims=True),
        ],
        axis=0,
    )

    @pl.when(step == pl.num_programs(0) - 1)
    def _():
        sq_ref[...] = pair_squares(gwq_ref[0], gwq_ref[1]) + pair_squares(gwo_ref[0], gwo_ref[1])


def branch_kernel(ao_ref, hb_ref, wo_ref, wdn_ref, br_ref):
    br_ref[...] = (dot_nn(ao_ref[...], wo_ref[...]) + dot_nn(hb_ref[...], wdn_ref[...])).astype(jnp.bfloat16)


def whole(shape):
    return pl.BlockSpec(shape, lambda *_: (0,) * len(shape))


def params(dims):
    return pltpu.CompilerParams(
        dimension_semantics=("arbitrary",) * dims, vmem_limit_bytes=VMEM_BYTES
    )


def dense(x_full, back_full, w_qkv, w_o, w_up, w_dn, norms, tables, seq_count, tile):
    rows, d = x_full.shape
    steps = rows // tile
    per_seq = steps // seq_count
    row = lambda width: pl.BlockSpec((tile, width), lambda s: (s, 0))
    table = pl.BlockSpec((tile, 128), lambda s: (lax.rem(s, per_seq), 0))
    act = lambda width: jax.ShapeDtypeStruct((rows, width), jnp.bfloat16)
    ff = w_up.shape[1]
    grad = jax.ShapeDtypeStruct((seq_count, ff, d), jnp.float32)
    grad_up = jax.ShapeDtypeStruct((seq_count, d, ff), jnp.float32)
    stat = jax.ShapeDtypeStruct((seq_count, 2, d), jnp.float32)
    squares = jax.ShapeDtypeStruct((3, d), jnp.float32)
    return pl.pallas_call(
        functools.partial(dense_kernel, per_seq),
        name="dense",
        grid=(steps,),
        in_specs=[row(d), row(d), whole(w_qkv.shape), whole(w_o.shape), whole(w_up.shape), whole(w_dn.shape),
                  whole(norms.shape), table, table, table],
        out_specs=[row(PART), row(PART), row(PART), row(PART), row(ff), row(d),
                   whole(grad.shape), whole(grad_up.shape), whole(stat.shape), whole(squares.shape)],
        out_shape=[act(PART), act(PART), act(PART), act(PART), act(ff), act(d), grad, grad_up, stat, squares],
        compiler_params=params(1),
    )(x_full, back_full, w_qkv, w_o, w_up, w_dn, norms, *tables)


def attend(q, k, v, d_out, tables, seq_count, block, heads):
    rows = q.shape[0]
    seq_len = rows // seq_count
    blocks = seq_len // block
    part = pl.BlockSpec((block, PART), lambda s, i: (s * blocks + i, 0))
    full = pl.BlockSpec((seq_len, PART), lambda s, i: (s, 0))
    act = jax.ShapeDtypeStruct((rows, PART), jnp.bfloat16)
    table = whole((seq_len, 128))
    return pl.pallas_call(
        functools.partial(attend_kernel, block, heads),
        name="attend",
        grid=(seq_count, blocks),
        in_specs=[part, full, full, part, table, table, table],
        out_specs=[part, part, full, full],
        out_shape=[act] * 4,
        scratch_shapes=[
            pltpu.VMEM((blocks, block, block), jnp.bfloat16),
            pltpu.VMEM((blocks + 1, block, 128), jnp.float32),
            pltpu.VMEM((block, 128), jnp.float32),
            pltpu.VMEM((block, PART), jnp.float32),
            pltpu.VMEM((block, PART), jnp.float32),
            pltpu.VMEM((seq_len, PART), jnp.float32),
            pltpu.VMEM((seq_len, PART), jnp.float32),
            pltpu.VMEM((block, PART), jnp.bfloat16),
            pltpu.VMEM((block, PART), jnp.bfloat16),
        ],
        compiler_params=params(2),
    )(q, k, v, d_out, *tables)


def grads(x_full, back_full, ao, dq, dk, dv, w_qkv, norms, seq_count, tile):
    rows, d = x_full.shape
    steps = rows // tile
    per_seq = steps // seq_count
    row = lambda width: pl.BlockSpec((tile, width), lambda s: (s, 0))
    grad_q = jax.ShapeDtypeStruct((seq_count, d, 3 * PART), jnp.float32)
    grad_o = jax.ShapeDtypeStruct((seq_count, PART, d), jnp.float32)
    stat = jax.ShapeDtypeStruct((seq_count, 2, d), jnp.float32)
    squares = jax.ShapeDtypeStruct((3, d), jnp.float32)
    return pl.pallas_call(
        functools.partial(grads_kernel, per_seq),
        name="grads",
        grid=(steps,),
        in_specs=[row(d), row(d), row(PART), row(PART), row(PART), row(PART), whole(w_qkv.shape), whole(norms.shape)],
        out_specs=[row(d), whole(grad_q.shape), whole(grad_o.shape), whole(stat.shape), whole(squares.shape)],
        out_shape=[jax.ShapeDtypeStruct((rows, d), jnp.bfloat16), grad_q, grad_o, stat, squares],
        compiler_params=params(1),
    )(x_full, back_full, ao, dq, dk, dv, w_qkv, norms)


def branch_of(ao, hb, w_o, w_dn, tile):
    rows = ao.shape[0]
    d = w_o.shape[1]
    row = lambda width: pl.BlockSpec((tile, width), lambda s: (s, 0))
    return pl.pallas_call(
        branch_kernel,
        name="branch",
        grid=(rows // tile,),
        in_specs=[row(ao.shape[1]), row(hb.shape[1]), whole(w_o.shape), whole(w_dn.shape)],
        out_specs=row(d),
        out_shape=jax.ShapeDtypeStruct((rows, d), jnp.bfloat16),
        compiler_params=params(1),
    )(ao, hb, w_o, w_dn)


def invert_kernel(slots_ref, out_ref):
    total = out_ref.shape[0]
    count = slots_ref.shape[0]
    wide = 16

    def clear(n, _):
        for u in range(wide):
            out_ref[n * wide + u] = -1
        return 0

    lax.fori_loop(0, total // wide, clear, 0)
    for n in range(total // wide * wide, total):
        out_ref[n] = -1

    def place(n, _):
        for u in range(wide):
            out_ref[slots_ref[n * wide + u]] = n * wide + u
        return 0

    lax.fori_loop(0, count // wide, place, 0)
    for n in range(count // wide * wide, count):
        out_ref[slots_ref[n]] = n


def invert(block_slot, total):
    return pl.pallas_call(
        invert_kernel,
        name="invert",
        in_specs=[pl.BlockSpec(memory_space=pltpu.SMEM)],
        out_specs=pl.BlockSpec(memory_space=pltpu.SMEM),
        out_shape=jax.ShapeDtypeStruct((total,), jnp.int32),
    )(block_slot)


def step_rates(position, d_model, inner_width, ff_local, seq_len):
    end_qkv = d_model * 3 * inner_width
    end_out = end_qkv + inner_width * d_model
    end_up = end_out + d_model * ff_local
    end_down = end_up + ff_local * d_model
    matrix_rate = d_model ** (-0.5)
    learn_rate = jnp.where(
        position < end_qkv,
        matrix_rate,
        jnp.where(
            position < end_out,
            (seq_len / (5.0 * d_model)) ** 0.5,
            jnp.where(position < end_up, matrix_rate, jnp.where(position < end_down, FF ** (-0.5), 0.1)),
        ),
    )
    weight_decay = jnp.where(position < end_down, 0.1, 0.0)
    return (learn_rate.astype(jnp.float32), weight_decay.astype(jnp.float32))


def on_device(tokens, cotangent, seq_group, block_slot, master, first_moment, second_moment):
    tensor_count = lax.axis_size("tensor")
    tensor_rank = lax.axis_index("tensor")
    owner_index = lax.axis_index("dp")
    owner_count = lax.axis_size("dp")
    local_rows, d = tokens.shape
    width_local = d // tensor_count
    heads_local = HEADS // tensor_count
    inner = heads_local * HD
    ff = FF // tensor_count
    seq_count = seq_group.shape[0]
    rows = local_rows * tensor_count
    seq_len = rows // seq_count
    capacity, block_width = master.shape[1:]
    block_count = block_slot.shape[0]
    slot_total = owner_count * capacity

    copies = lax.all_gather(master[0].astype(jnp.bfloat16), "dp", axis=0, tiled=True)
    slot_block = invert(block_slot, slot_total)
    x_full = lax.all_gather(tokens, "tensor", axis=0, tiled=True)
    back_full = lax.all_gather(cotangent, "tensor", axis=0, tiled=True)
    flat = copies[block_slot].reshape(-1)
    end_qkv = d * 3 * inner
    end_out = end_qkv + inner * d
    end_up = end_out + d * ff
    end_down = end_up + ff * d
    w_qkv = jnp.pad(flat[:end_qkv].reshape(d, 3, inner), ((0, 0), (0, 0), (0, PART - inner))).reshape(d, 3 * PART)
    w_o = jnp.pad(flat[end_qkv:end_out].reshape(inner, d), ((0, PART - inner), (0, 0)))
    w_up = flat[end_out:end_up].reshape(d, ff)
    w_dn = flat[end_up:end_down].reshape(ff, d)
    norm_rows_all = lax.all_gather(flat[end_down:].reshape(1, 4, width_local), "tensor", axis=0, tiled=True)
    norms = jnp.transpose(norm_rows_all, (1, 0, 2)).reshape(4, d).astype(jnp.float32)
    tables = turn_tables(seq_len)

    q, k, v, d_out, hidden, second_back, grad_down, grad_up, stat_two, squares_two = dense(
        x_full, back_full, w_qkv, w_o, w_up, w_dn, norms, tables, seq_count, 256
    )
    second_sum = lax.psum_scatter(second_back, "tensor", scatter_dimension=0, tiled=True)
    mixed, dq, dk, dv = attend(q, k, v, d_out, tables, seq_count, 512, heads_local)
    first_back, grad_qkv, grad_o, stat_one, squares_one = grads(
        x_full, back_full, mixed, dq, dk, dv, w_qkv, norms, seq_count, 256
    )
    branch = branch_of(mixed, hidden, w_o, w_dn, 512)

    local_squares = jnp.sum(squares_one + squares_two, axis=1)
    stats = jnp.concatenate([stat_one, stat_two], axis=1)
    packed = lax.psum(jnp.concatenate([stats.reshape(-1), local_squares]), "tensor")
    stats = packed[:-3].reshape(seq_count, 4, d)
    local_squares = packed[-3:]
    same = seq_group[0] == seq_group[1]
    stat_both = jnp.sum((stats[0] + stats[1]) ** 2)
    stat_each = jnp.sum(stats * stats, axis=(1, 2))
    each = local_squares[1:] + stat_each
    both = local_squares[0] + stat_both
    groups = jnp.arange(seq_count, dtype=jnp.int32)
    held = (seq_group[None, :] == groups[:, None]).astype(jnp.float32)
    sole = held[:, 0] * each[0] + held[:, 1] * each[1]
    norm_squares = jnp.where(held[:, 0] * held[:, 1] > 0, both, sole)
    group_norms = jnp.sqrt(norm_squares)
    clip = 1.0 / jnp.maximum(group_norms, 1.0)
    c = clip[seq_group]
    mix = lambda g: c[0] * g[0] + c[1] * g[1]
    own_stats = lax.dynamic_slice_in_dim(stats, tensor_rank * width_local, width_local, 2)
    clipped = jnp.concatenate(
        [
            mix(grad_qkv).reshape(d, 3, PART)[:, :, :inner].reshape(-1),
            mix(grad_o)[:inner].reshape(-1),
            mix(grad_up).reshape(-1),
            mix(grad_down).reshape(-1),
            mix(own_stats).reshape(-1),
        ]
    ).astype(jnp.bfloat16).reshape(block_count, block_width)
    padded = -(-capacity // 16) * 16
    wanted = jnp.pad(slot_block.reshape(owner_count, capacity), ((0, 0), (0, padded - capacity)), constant_values=-1)
    in_slots = clipped[jnp.maximum(wanted.reshape(-1), 0)]
    owned = lax.psum_scatter(in_slots, "dp", scatter_dimension=0, tiled=True)[:capacity].astype(jnp.float32)
    my_blocks = lax.dynamic_slice_in_dim(slot_block, owner_index * capacity, capacity)
    owned = jnp.where(my_blocks[:, None] >= 0, owned, 0.0)
    position = jnp.maximum(my_blocks, 0)[:, None] * block_width + jnp.arange(block_width, dtype=jnp.int32)[None, :]
    learn_rate, weight_decay = step_rates(position, d, inner, ff, seq_len)
    new_one = beta_one * first_moment[0] + (1.0 - beta_one) * owned
    new_two = beta_two * second_moment[0] + (1.0 - beta_two) * owned * owned
    new_weight = master[0] - learn_rate * (new_one / (jnp.sqrt(new_two) + eps_adam) + weight_decay * master[0])

    branch_sum = lax.psum_scatter(branch, "tensor", scatter_dimension=0, tiled=True).astype(jnp.float32)
    output = (tokens.astype(jnp.float32) + branch_sum).astype(jnp.bfloat16)
    first_sum = lax.psum_scatter(first_back, "tensor", scatter_dimension=0, tiled=True).astype(jnp.float32)
    second_sum = second_sum.astype(jnp.float32)
    own = tokens.astype(jnp.float32)
    centred = own - jnp.mean(own, axis=-1, keepdims=True)
    inverse = lax.rsqrt(jnp.mean(centred * centred, axis=-1, keepdims=True) + eps_norm)
    xhat = centred * inverse
    grad_input = cotangent.astype(jnp.float32)
    for total, gain in ((first_sum, norms[0]), (second_sum, norms[2])):
        scaled = total * gain
        mean = jnp.mean(scaled, axis=1, keepdims=True)
        cross = jnp.mean(scaled * xhat, axis=1, keepdims=True)
        grad_input = grad_input + inverse * (scaled - mean - xhat * cross)
    return (output, grad_input, group_norms, new_weight[None], new_one[None], new_two[None])


def solution(mesh):
    rows = P(("dp", "tensor"), None)
    slots = P("tensor", "dp", None)
    return jax.shard_map(
        on_device,
        mesh=mesh,
        in_specs=(rows, rows, P("dp"), P(), slots, slots, slots),
        out_specs=(rows, rows, P("dp"), slots, slots, slots),
        check_vma=False,
    )
```

time: 1460 us -> 820 us (0.56)
  matrix products: 624 us -> 0 us
  Pallas kernels: 0 us -> 268 us
  other arithmetic: 172 us -> 40.5 us
  local copies, waits for them, and re-layouts: 273 us -> 156 us
  waiting for transfers between devices: 339 us -> 314 us
  loops' own time: 16.5 us -> 0 us
    dot_general x46 -> x0, matrix products: 624 us -> none  [the longest x1 119 us: on_device(): clipped = jnp.dot(clip_scale, group_grads, precision=lax.Precision.HIGHEST)]
    pallas_call x0 -> x5, Pallas kernels: none -> 268 us  [the longest x1 139 us: attend(): pl.pallas_call(functools.partial(attend_kernel, block, heads), name='atte...]
    reduce_scatter x3 -> x4, waiting for transfers between devices: 21.3 us -> 236 us  [the longest x1 88.3 us: on_device(): lax.psum_scatter(in_slots, 'dp', scatter_dimension=0, tiled=True)[:capacity]]
    psum x1 -> x0, waiting for transfers between devices: 158 us -> none  [on_device(): summed = lax.psum(grad_rows, 'dp')]
    all_gather x1, waiting for transfers between devices: 149 us -> 41.8 us  [on_device(): lax.all_gather(master[0].astype(jnp.bfloat16), 'dp', axis=0, tiled=True)]
    convert_element_type x8 -> x2, other arithmetic: 77.7 us -> 0.07 us  [the longest x1 0.07 us: on_device(): held = (seq_group[None, :] == groups[:, None]).astype(jnp.float32)]
    scatter x1 -> x0, local copies, waits for them, and re-layouts: 65.6 us -> none  [on_device(): slot_block = jnp.full((slot_total,), -1, jnp.int32).at[block_slot].set(jn...]
    reduce_sum x7 -> x6, other arithmetic: 57.3 us -> 5.79 us  [the longest x1 3.38 us: on_device(): cross = jnp.mean(scaled * xhat, axis=1, keepdims=True)]
  transfers between devices with their start and end apart: 8 -> 7, of which waited for: 4 -> 6; matrix products, arithmetic and copies ran while one was open for 31% -> 12% of each run, Pallas kernels for 0% -> 7%
where the time goes in v1:
time: 820 us; the launch traced here: 811 us
  waiting for transfers between devices  314 us (38%)
  Pallas kernels  268 us (33%)
  local copies, waits for them, and re-layouts  156 us (19%)
  other arithmetic  40.5 us (5%)
  between operations  16.3 us (2%)
  blocking collectives  15.7 us (2%)
    pallas_call x1, Pallas kernels, attend(): pl.pallas_call(functools.partial(attend_kernel, block, heads), name='atte...  139 us
    reduce_scatter x1, waiting for transfers between devices, on_device(): lax.psum_scatter(in_slots, 'dp', scatter_dimension=0, tiled=True)[:capacity]  88.3 us
    reduce_scatter x1, waiting for transfers between devices, on_device(): lax.psum_scatter(first_back, 'tensor', scatter_dimension=0, tiled=True)  61.3 us
    reduce_scatter x1, waiting for transfers between devices, on_device(): lax.psum_scatter(branch, 'tensor', scatter_dimension=0, tiled=True)  58 us
    pallas_call x1, Pallas kernels, dense(): pl.pallas_call(functools.partial(dense_kernel, per_seq), name='dense', gr...  50.2 us
    gather x1, local copies, waits for them, and re-layouts, on_device(): in_slots = clipped[jnp.maximum(wanted.reshape(-1), 0)]  46.6 us
    unnamed x36, local copies, waits for them, and re-layouts  42.2 us
    all_gather x1, waiting for transfers between devices, on_device(): lax.all_gather(master[0].astype(jnp.bfloat16), 'dp', axis=0, tiled=True)  41.8 us
  transfers between devices with their start and end apart: 7, of which 6 were waited for; matrix products, arithmetic and copies ran while one was open for 12% of the time, Pallas kernels for 7%

profile of v1, /device:TPU:0, one launch (start us, length us, event | category | flops | bytes accessed | tf_op | source)
XLA Modules:
  0.0 811.1 jit_solution(507019269987897441)
XLA Ops:
  7.2 2.2 copy.85
  9.5 0.7 all-gather.5.cloned.1.call-update
  10.3 0.7 all-gather.7.cloned.1.call-update
  11.8 1.3 copy.53.keep_ref
  13.2 1.3 copy.54.low_ref
  14.7 1.4 copy.55.high_ref
  16.0 40.1 %invert.1 = s32[20752]{0:T(1024)} custom-call(s32[13830]{0:T(1024)} %slots_ref.1), custom_call_target="tpu_custom_call" | custom-call | tf_op jit(solution)/shard_map/invert/pallas_call | solution.py:382
  56.1 1.0 reshape.204
  57.4 0.6 pad_clamp_fusion.1
  58.0 0.7 pad_clamp_fusion
  58.6 41.8 %all-gather.9.cloned.1.call-done = bf16[8,2594,128]{2,1,0:T(8,128)(2,1)} async-done(((bf16[1,2594,128]{2,1,0:T(8,128)(2,1)}), bf16[8,2594,128]{2,1,0:T(8,128)(2,1)}) %all-gather.9.cloned.1.call-update) | async-done | bytes 5312528 | tf_op jit(solution)/shard_map/all_gather | solution.py:427
  100.4 4.8 reshape.233
  105.2 30.3 %gather_fusion = bf16[13830,128]{1,0:T(8,128)(2,1)S(1)} fusion(bf16[20752,128]{1,0:T(8,128)(2,1)} %reshape.233, s32[14336]{0:T(1024)} %pad_clamp_fusion.1), kind=kCustom, calls=%fused_computation | custom fusion | bytes 7136280 | tf_op jit(solution)/shard_map/gather | solution.py:431
  135.5 1.0 slice.161
  136.6 4.6 reshape.194
  141.2 3.4 copy.68
  144.6 1.3 pad.12.clone
  145.9 1.5 copy.52.wqkv_ref
  147.6 0.8 pad.13.wo_ref
  148.4 1.8 fusion.41
  150.2 1.9 reshape.197.wup_ref
  152.0 1.9 reshape.198.wdn_ref
  154.0 5.3 all_gather.15
  159.3 0.6 copy-done.8
  159.9 0.7 convert_element_type.48.nrm_ref
  160.6 33.9 %all-gather.7.cloned.1.call-done.g_ref = bf16[4096,768]{1,0:T(8,128)(2,1)} async-done(((bf16[1024,768]{1,0:T(8,128)(2,1)}), bf16[4096,768]{1,0:T(8,128)(2,1)}) %all-gather.7.cloned.1.call-update) | async-done | bytes 6291472 | tf_op jit(solution)/shard_map/all_gather | solution.py:430
  194.5 50.2 %dense.1 = (bf16[4096,256]{1,0:T(8,128)(2,1)}, bf16[4096,256]{1,0:T(8,128)(2,1)}, bf16[4096,256]{1,0:T(8,128)(2,1)}, bf16[4096,256]{1,0:T(8,128)(2,1)}, bf16[409...) custom-call(bf16[4096,768]{1,0:T(8,128)(2,1)} %all-gather.5.cloned.1, ...), custom_call_target="tpu_custom_call" | custom-call | tf_op jit(solution)/shard_map/dense/pallas_call | solution.py:279
  244.7 139.0 %attend.1 = (bf16[4096,256]{1,0:T(8,128)(2,1)}, bf16[4096,256]{1,0:T(8,128)(2,1)}, bf16[4096,256]{1,0:T(8,128)(2,1)}, bf16[4096,256]{1,0:T(8,128)(2,1)}) custom-call(bf16[4096,256]{1,0:T(8,128)(2,1)} %get-tuple-element.25.q_ref, bf16[4096,256]{1,0:T(8,128)(2,1)} %get-tuple-element.26.k_ref, bf16[4096,256]{1,0:T(8,128)(2,1)} %get-tuple-element.27.v_ref, ...), custom_call_target="tpu_custom_call" | custom-call | tf_op jit(solution)/shard_map/attend/pallas_call | solution.py:300
  383.8 26.4 %grads.1 = (bf16[4096,768]{1,0:T(8,128)(2,1)}, f32[2,768,768]{2,1,0:T(8,128)}, f32[2,256,768]{2,1,0:T(8,128)}, f32[2,2,768]{2,1,0:T(2,128)}, f32[3,768]{1,0:T(4,128)}) custom-call(bf16[4096,768]{1,0:T(8,128)(2,1)} %all-gather.5.cloned.1.call-done.x_ref, bf16[4096,768]{1,0:T(8,128)(2,1)} %all-gather.7.cloned.1.call-done.g_ref, ...), custom_call_target="tpu_custom_call" | custom-call | tf_op jit(solution)/shard_map/grads/pallas_call | solution.py:331
  410.2 0.7 pad_maximum_fusion.2
  410.9 0.8 add_reduce_fusion
  411.8 10.4 %psum.7 = f32[6147]{0:T(1024)S(1)} all-reduce(f32[6147]{0:T(1024)S(1)} %pad_maximum_fusion.1), channel_id=1, replica_groups=mesh['dp'=8,'tensor'=4] {'tensor'}, use_global_device_ids=true, to_apply=%region_10.11 | all-reduce | flops 6147 | bytes 49176 | tf_op jit(solution)/shard_map/psum | solution.py:456
  422.7 0.6 fusion.35
  425.4 1.8 maximum_divide_fusion
  427.2 0.6 gather_fusion.1
  428.4 3.9 add_convert_fusion.2
  432.4 0.6 copy.60
  433.1 1.0 copy.61
  434.1 2.5 reshape.202
  436.6 1.3 constant_dynamic-update-slice_fusion.4
  438.3 2.0 fusion.31
  440.4 1.9 reshape.203
  442.3 4.9 add_convert_fusion.1
  447.2 3.3 add.152
  450.6 4.9 add_convert_fusion
  455.5 3.3 add.154
  458.9 2.0 fusion.37
  461.0 1.1 constant_dynamic-update-slice_fusion.3
  462.1 1.3 constant_dynamic-update-slice_fusion.2
  463.5 46.6 %gather_fusion.2 = bf16[20864,128]{1,0:T(8,128)(2,1)} fusion(bf16[13830,128]{1,0:T(8,128)(2,1)S(1)} %bitcast.54, s32[21504]{0:T(1024)} %pad_clamp_fusion), kind=kCustom, calls=%fused_computation.2 | custom fusion | bytes 10765824 | tf_op jit(solution)/shard_map/gather | solution.py:484
  511.4 12.7 %branch.1 = bf16[4096,768]{1,0:T(8,128)(2,1)} custom-call(bf16[4096,256]{1,0:T(8,128)(2,1)} %get-tuple-element.29.ao_ref, bf16[4096,768]{1,0:T(8,128)(2,1)} %get-tuple-element.30.hb_ref, bf16[256,768]{1,0:T(8,128)(2,1)} %pad.13.wo_ref, bf16[768,768]{1,0:T(8,128)(2,1)} %reshape.198.wdn_ref), custom_call_target="tpu_custom_call" | custom-call | tf_op jit(solution)/shard_map/branch/pallas_call | solution.py:346
  524.1 1.0 dynamic-slice_compare_fusion
  525.1 0.8 maximum_multiply_fusion
  526.2 0.6 fusion.14
  527.0 88.3 %reduce-scatter.11.cloned.1.call-done = bf16[2608,128]{1,0:T(8,128)(2,1)} async-done(((bf16[20864,128]{1,0:T(8,128)(2,1)}), bf16[2608,128]{1,0:T(8,128)(2,1)}) %reduce-scatter.11.cloned.1.call-update) | async-done | bytes 667664 | tf_op jit(solution)/shard_map/reduce_scatter | solution.py:485
  615.3 5.3 fusion.29
  620.6 9.0 %copy.63 = f32[1,2594,128]{2,0,1:T(1,128)} copy(f32[1,2594,128]{2,1,0:T(8,128)S(1)} %get-tuple-element.79) | data formatting | bytes 2656256
  629.6 9.0 %copy.64 = f32[1,2594,128]{2,0,1:T(1,128)} copy(f32[1,2594,128]{2,1,0:T(8,128)S(1)} %get-tuple-element.80) | data formatting | bytes 2656256
  638.6 9.0 %copy.65 = f32[1,2594,128]{2,0,1:T(1,128)} copy(f32[1,2594,128]{2,1,0:T(8,128)S(1)} %get-tuple-element.78) | data formatting | bytes 2656256
  647.6 28.3 %reduce-scatter.9.cloned.1.call-done = bf16[1024,768]{1,0:T(8,128)(2,1)} async-done(((bf16[4096,768]{1,0:T(8,128)(2,1)}), bf16[1024,768]{1,0:T(8,128)(2,1)}) %reduce-scatter.9.cloned.1.call-update) | async-done | bytes 1572880 | tf_op jit(solution)/shard_map/reduce_scatter | solution.py:447
  675.9 61.3 %reduce-scatter.7.cloned.1.call-done = bf16[1024,768]{1,0:T(8,128)(2,1)} async-done(((bf16[4096,768]{1,0:T(8,128)(2,1)}), bf16[1024,768]{1,0:T(8,128)(2,1)}) %reduce-scatter.7.cloned.1.call-update) | async-done | bytes 1572880 | tf_op jit(solution)/shard_map/reduce_scatter | solution.py:496
  737.1 3.4 fusion.6
  740.6 58.0 %reduce-scatter.5.cloned.1.call-done = bf16[1024,768]{1,0:T(8,128)(2,1)} async-done(((bf16[4096,768]{1,0:T(8,128)(2,1)}), bf16[1024,768]{1,0:T(8,128)(2,1)}) %reduce-scatter.5.cloned.1.call-update) | async-done | bytes 1572880 | tf_op jit(solution)/shard_map/reduce_scatter | solution.py:494
  798.5 5.2 fusion.10
  (87 shorter events, 6.0 us)
Async XLA Ops:
  7.2 93.2 %all-gather.9.cloned.1.call-start = ((), (), s32[]{:S(2)}) async-start(), calls=%async_computation.10 | async-start | bytes 5990400 | tf_op jit(solution)/shard_map/all_gather | solution.py:427
  9.5 151.2 %all-gather.5.cloned.1.call-start = ((), (), s32[]{:S(2)}) async-start(), calls=%async_computation.4 | async-start | bytes 7864320 | tf_op jit(solution)/shard_map/all_gather | solution.py:429
  10.2 184.3 %all-gather.7.cloned.1.call-start = ((), (), s32[]{:S(2)}) async-start(), calls=%async_computation.5 | async-start | bytes 7864320 | tf_op jit(solution)/shard_map/all_gather | solution.py:430
  11.0 604.4 %reduce-scatter.11.cloned.1.call-start = ((), (), s32[]{:S(2)}) async-start(), calls=%async_computation.9 | async-start | bytes 6008832 | tf_op jit(solution)/shard_map/reduce_scatter | solution.py:485
  14.5 42.7 %copy-start.12 = (s32[2]{0:T(128)S(1)}, s32[2]{0:T(128)}, u32[]{:S(2)}) copy-start(s32[2]{0:T(128)} %param.9) | copy-start | bytes 28
  14.5 42.8 %copy-start.6 = (s32[13830]{0:T(1024)S(1)}, s32[13830]{0:T(1024)}, u32[]{:S(2)}) copy-start(s32[13830]{0:T(1024)} %slots_ref.1) | copy-start | bytes 165964
  135.5 5.6 copy-start.1
  144.6 2.8 slice-start
  150.2 3.7 slice-start.1
  159.3 0.6 copy-start.8
  383.8 26.4 %copy-start.11 = (f32[2,2,768]{2,1,0:T(2,128)S(1)}, f32[2,2,768]{2,1,0:T(2,128)}, u32[]{:S(2)}) copy-start(f32[2,2,768]{2,1,0:T(2,128)} %get-tuple-element.37) | copy-start | bytes 36868
  383.8 27.1 %copy-start.10 = (f32[3,768]{1,0:T(4,128)S(1)}, f32[3,768]{1,0:T(4,128)}, u32[]{:S(2)}) copy-start(f32[3,768]{1,0:T(4,128)} %get-tuple-element.39) | copy-start | bytes 27652
  423.3 5.1 copy-start.7
  436.6 1.7 copy-start.5
  461.0 2.4 copy-start.4
  510.1 165.7 %reduce-scatter.9.cloned.1.call-start = ((), (), s32[]{:S(2)}) async-start(), calls=%async_computation.8 | async-start | bytes 7864320 | tf_op jit(solution)/shard_map/reduce_scatter | solution.py:447
  510.7 226.4 %reduce-scatter.7.cloned.1.call-start = ((), (), s32[]{:S(2)}) async-start(), calls=%async_computation.7 | async-start | bytes 7864320 | tf_op jit(solution)/shard_map/reduce_scatter | solution.py:496
  511.3 287.2 %reduce-scatter.5.cloned.1.call-start = ((), (), s32[]{:S(2)}) async-start(), calls=%async_computation.6 | async-start | bytes 7864320 | tf_op jit(solution)/shard_map/reduce_scatter | solution.py:494
  524.1 1.8 copy-start
  524.1 2.7 copy-start.9
  524.1 91.2 %copy-start.3 = (f32[1,2594,128]{2,0,1:T(1,128)S(1)}, f32[1,2594,128]{2,0,1:T(1,128)}, u32[]{:S(2)}) copy-start(f32[1,2594,128]{2,0,1:T(1,128)} %param.11) | copy-start | bytes 3984388
  647.6 151.0 %copy-start.2 = (bf16[1024,768]{1,0:T(8,128)(2,1)S(1)}, bf16[1024,768]{1,0:T(8,128)(2,1)}, u32[]{:S(2)}) copy-start(bf16[1024,768]{1,0:T(8,128)(2,1)} %param.8) | copy-start | bytes 4718596
Sparse Core Ops, SparseCore 0:
  10.7 89.6 all-gather.8
  102.0 44.5 all-gather.4
  148.1 46.3 all-gather.6
  510.3 105.0 reduce-scatter.10
  617.7 58.1 reduce-scatter.8
  678.3 58.8 reduce-scatter.6
  739.7 58.8 reduce-scatter.4
